TPU v7x, 32 devices: a whole 2x2x4 slice. The times are simulated.
32 devices in a mesh: ctx: 8 (over y, x, core), pipe: 4 (over z).
Axes of the slice: x: 2, y: 2, z: 4, core: 2. Of those that a mesh axis runs over, the one named last changes fastest.
Arguments:
- tokens: bfloat16 [1, 1024, 2048], P(None, 'ctx'), may hold values from -6 to 6
- w_qkv: bfloat16 [4, 16, 128, 384], P('pipe'), may hold values from -0.5 to 0.5
- norm_gain: float32 [4, 2048], P('pipe'), may hold values from 0.5 to 1.5
- out_gain: float32 [4, 2048], P('pipe'), may hold values from 0.5 to 1.5
Outputs:
- hidden: bfloat16 [4, 1, 1024, 2048], P('pipe', None, 'ctx')
All inputs are finite; a program needn't handle non-finite values.
Results may differ from a plain program's by a relative error of at most 0.03.
Values may be sent and summed in bfloat16 or wider, within the bound.
A program may use at most 128 MiB of HBM per device.

v0:
```python
import functools

import jax
import jax.numpy as jnp
from jax import lax
from jax.experimental import pallas as pl
from jax.experimental.pallas import tpu as pltpu
from jax.sharding import PartitionSpec as P

epsilon = 1e-06


def shifted(block, axis, distance):
    devices = range(lax.axis_size(axis))
    route = [(i - distance, i) for i in devices if i - distance in devices]
    return lax.ppermute(block, axis, route)


def run_layer(stream, gain_in, weights, gain_out):
    row_count = stream.shape[0]
    head_count = weights.shape[0]
    head_dim = weights.shape[1]
    widened = stream.astype(jnp.float32)
    normed = (
        widened * lax.rsqrt(jnp.mean(widened * widened, -1, keepdims=True) + epsilon) * gain_in
    ).astype(jnp.bfloat16)
    projected = jnp.einsum(
        "thd,hde->hte",
        normed.reshape(row_count, head_count, head_dim),
        weights,
        preferred_element_type=jnp.float32,
    )
    queries = (projected[..., :head_dim] * head_dim ** (-0.5)).astype(jnp.bfloat16)
    keys_local = projected[..., head_dim : 2 * head_dim].astype(jnp.bfloat16)
    values_local = projected[..., 2 * head_dim :].astype(jnp.bfloat16)
    kv_state = jnp.einsum(
        "hte,htf->hef", keys_local, values_local, preferred_element_type=jnp.float32
    )
    flat_state = kv_state.reshape(1, head_count * head_dim, head_dim)
    spread = lax.all_to_all(
        flat_state.astype(jnp.bfloat16), "ctx", split_axis=1, concat_axis=0, tiled=True
    ).astype(flat_state.dtype)
    running = jnp.cumsum(spread, axis=0)
    lower = jnp.concatenate([jnp.zeros_like(spread[:1]), running[:-1]], axis=0)
    returned = lax.all_to_all(
        lower.astype(jnp.bfloat16), "ctx", split_axis=0, concat_axis=1, tiled=True
    ).astype(lower.dtype)
    prefix = returned.reshape(kv_state.shape)
    scores = jnp.einsum("hte,hse->hts", queries, keys_local, preferred_element_type=jnp.float32)
    positions = jnp.arange(row_count, dtype=jnp.int32)
    causal = positions[:, None] >= positions[None, :]
    masked = jnp.where(causal, scores, 0.0).astype(jnp.bfloat16)
    mixed_heads = jnp.einsum(
        "hts,hsf->htf", masked, values_local, preferred_element_type=jnp.float32
    )
    mixed_heads = mixed_heads + jnp.einsum(
        "hte,hef->htf", queries, prefix.astype(jnp.bfloat16), preferred_element_type=jnp.float32
    )
    mixed_heads = mixed_heads * lax.rsqrt(
        jnp.mean(mixed_heads * mixed_heads, -1, keepdims=True) + epsilon
    )
    branch = jnp.transpose(mixed_heads, (1, 0, 2)).reshape(row_count, head_count * head_dim)
    return (widened + branch * gain_out).astype(jnp.bfloat16)


def shards(tokens, w_qkv, norm_gain, out_gain):
    section_count = lax.axis_size("pipe")
    section_index = lax.axis_index("pipe")
    micro_count = tokens.shape[0]
    hidden_buffer = jnp.zeros(tokens.shape, jnp.bfloat16)
    carried = jnp.zeros(tokens.shape[1:], jnp.bfloat16)
    total_steps = micro_count + section_count - 1
    for tick_index in range(total_steps):
        fresh = tokens[min(tick_index, micro_count - 1)]
        layer_input = jnp.where(section_index == 0, fresh, carried)
        result = run_layer(layer_input, norm_gain[0], w_qkv[0], out_gain[0])
        micro_index = tick_index - section_index
        usable = (micro_index >= 0) & (micro_index < micro_count)
        slot_index = jnp.clip(micro_index, 0, micro_count - 1)
        previous = lax.dynamic_index_in_dim(hidden_buffer, slot_index, 0, keepdims=False)
        hidden_buffer = lax.dynamic_update_index_in_dim(
            hidden_buffer, jnp.where(usable, result, previous), slot_index, 0
        )
        if tick_index + 1 < total_steps:
            carried = shifted(result, "pipe", 1)
    return hidden_buffer[None]


MESH = pl.DeviceIdType.MESH
FAR_FIRST = (6, 7, 2, 4, 3, 5, 1)


def partner(index, flips):
    total = 0
    for bit in (1, 2, 4):
        own = lax.rem(index // bit, 2)
        total = total + (lax.rem(own + 1, 2) if flips & bit else own) * bit
    return total


def lanes_to_rows(row):
    return jnp.broadcast_to(row, (128, row.shape[1])).T


def row_sums(values):
    upper = values.astype(jnp.bfloat16)
    lower = (values - upper.astype(jnp.float32)).astype(jnp.bfloat16)
    ones = jnp.ones((256, 128), jnp.bfloat16)
    return jnp.dot(
        jnp.concatenate([upper, lower], 1), ones, preferred_element_type=jnp.float32
    )


def relay_kernel(
    sizes,
    tok_ref,
    w_ref,
    gin_ref,
    gout_ref,
    out_ref,
    own,
    stream,
    weights,
    gains_in,
    gains_out,
    qkv,
    prefix,
    squares,
    local_sem,
    tok_send,
    tok_recv,
    sq_send,
    sq_recv,
    w_send,
    w_recv,
    out_send,
    out_recv,
):
    ctx_size, sections, heads, dim, tokens = sizes
    width = heads * dim
    features = ctx_size * width
    c = lax.axis_index("ctx")
    z = lax.axis_index("pipe")

    def cols(device):
        return pl.ds(pl.multiple_of(device * width, width), width)

    def rows(device):
        return pl.ds(pl.multiple_of(device * tokens, tokens), tokens)

    my_heads = pl.ds(c * heads, heads)

    local = [
        pltpu.make_async_copy(tok_ref.at[0], own, local_sem.at[0]),
        pltpu.make_async_copy(tok_ref.at[0, :, cols(c)], stream.at[rows(c)], local_sem.at[1]),
        pltpu.make_async_copy(w_ref.at[0, my_heads], weights.at[z], local_sem.at[2]),
        pltpu.make_async_copy(gin_ref.at[:, cols(c)], gains_in.at[z], local_sem.at[3]),
        pltpu.make_async_copy(gout_ref.at[:, cols(c)], gains_out.at[z], local_sem.at[4]),
    ]
    for copy in local:
        copy.start()

    barrier = pltpu.get_barrier_semaphore()
    for d in FAR_FIRST:
        pl.semaphore_signal(barrier, 1, device_id=(partner(c, d), z), device_id_type=MESH)
    for step in range(1, sections):
        other = lax.rem(z + step, sections)
        pl.semaphore_signal(barrier, 1, device_id=(c, other), device_id_type=MESH)
    pl.semaphore_wait(barrier, ctx_size + sections - 2)

    def tok_copy(d):
        to = partner(c, d)
        return pltpu.make_async_remote_copy(
            tok_ref.at[0, :, cols(to)], stream.at[rows(c)],
            tok_send.at[d], tok_recv.at[d], device_id=(to, z), device_id_type=MESH,
        )

    def sq_copy(layer, d):
        return pltpu.make_async_remote_copy(
            squares.at[layer, c], squares.at[layer, c],
            sq_send.at[layer, d], sq_recv.at[layer, d],
            device_id=(partner(c, d), z), device_id_type=MESH,
        )

    def w_copies(layer, to, slot, relayed):
        pieces = (
            (weights.at[layer], weights.at[layer]) if relayed else (w_ref.at[0, my_heads], weights.at[layer]),
            (gains_in.at[layer], gains_in.at[layer]) if relayed else (gin_ref.at[:, cols(c)], gains_in.at[layer]),
            (gains_out.at[layer], gains_out.at[layer]) if relayed else (gout_ref.at[:, cols(c)], gains_out.at[layer]),
        )
        return [
            pltpu.make_async_remote_copy(
                source, target, w_send.at[slot, i], w_recv.at[layer, i],
                device_id=(c, to), device_id_type=MESH,
            )
            for i, (source, target) in enumerate(pieces)
        ]

    last = sections - 1
    plan = {"start": [], "early": [], "late": [], "relay": []}
    plan["start"].append((0, 0, last, 0))
    for layer in range(1, last - 1):
        plan["early"].append((layer, layer, last, 0))
    plan["late"].append((last - 1, last - 1, last, 0))
    for layer in range(last - 1):
        for slot, to in enumerate(range(layer + 1, last)):
            if not (layer == 0 and to == last - 1 and last > 2):
                plan["late"].append((layer, layer, to, slot + 1))
    if last > 2:
        plan["relay"].append((last, 0, last - 1, 0))

    def send_weights(stage):
        for sender, layer, to, slot in plan[stage]:
            @pl.when(z == sender)
            def _():
                for copy in w_copies(layer, to, slot, stage == "relay"):
                    copy.start()

    send_weights("start")
    for d in FAR_FIRST:
        tok_copy(d).start()

    local[0].wait()
    folded = jnp.zeros((tokens, 128), jnp.float32)
    for i in range(features // 128):
        piece = own[:, i * 128 : (i + 1) * 128].astype(jnp.float32)
        folded = folded + piece * piece
    total = jnp.sum(folded.T, 0, keepdims=True)
    which = lax.broadcasted_iota(jnp.int32, (ctx_size, tokens), 0)
    squares[0, c] = jnp.where(which == c, jnp.broadcast_to(total, (ctx_size, tokens)), 0.0)
    for d in FAR_FIRST:
        sq_copy(0, d).start()
    for d in FAR_FIRST[:2]:
        tok_copy(d).wait_recv()
    send_weights("early")
    for d in FAR_FIRST[2:]:
        tok_copy(d).wait_recv()
    for copy in local[1:]:
        copy.wait()
    send_weights("late")

    at_row = lax.broadcasted_iota(jnp.int32, (tokens, tokens), 0)
    at_col = lax.broadcasted_iota(jnp.int32, (tokens, tokens), 1)
    causal = at_row >= at_col

    def out_copy(d):
        to = partner(c, d)
        return pltpu.make_async_remote_copy(
            stream.at[rows(to)], out_ref.at[0, 0, :, cols(c)],
            out_send.at[d], out_recv.at[d], device_id=(to, z), device_id_type=MESH,
        )

    def own_out():
        return pltpu.make_async_copy(
            stream.at[rows(c)], out_ref.at[0, 0, :, cols(c)], local_sem.at[0]
        )

    def one_layer(layer, carry):
        @pl.when(layer < z)
        def _():
            for copy in w_copies(layer, z, 0, True):
                copy.wait_recv()

        @pl.when(layer == 0)
        def _():
            send_weights("relay")

        for d in FAR_FIRST:
            sq_copy(layer, d).wait_recv()
        scale = lax.rsqrt(jnp.sum(squares[layer], 0) * (1.0 / features) + epsilon)
        running = [jnp.zeros((dim, dim), jnp.float32) for _ in range(heads)]
        for block in range(ctx_size):
            here = slice(block * tokens, (block + 1) * tokens)
            by_row = lanes_to_rows(scale[block : block + 1, :])
            for h in range(heads):
                mine = slice(h * dim, (h + 1) * dim)
                normed = (
                    stream[here, mine].astype(jnp.float32) * by_row * gains_in[layer, :, mine]
                ).astype(jnp.bfloat16)
                projected = jnp.dot(
                    normed, weights[layer, h], preferred_element_type=jnp.float32
                )
                keys = projected[:, dim : 2 * dim].astype(jnp.bfloat16)
                values = projected[:, 2 * dim :].astype(jnp.bfloat16)
                qkv[h, here, :dim] = (projected[:, :dim] * dim ** (-0.5)).astype(jnp.bfloat16)
                qkv[h, here, dim : 2 * dim] = keys
                qkv[h, here, 2 * dim :] = values
                prefix[h, block] = running[h].astype(jnp.bfloat16)
                if block + 1 < ctx_size:
                    running[h] = running[h] + lax.dot_general(
                        keys, values, (((0,), (0,)), ((), ())),
                        preferred_element_type=jnp.float32,
                    )
        for d in FAR_FIRST + (0,):
            block = partner(c, d)
            here = rows(block)
            folded = jnp.zeros((tokens, dim), jnp.float32)
            for h in range(heads):
                mine = slice(h * dim, (h + 1) * dim)
                queries = qkv[h, here, :dim]
                values = qkv[h, here, 2 * dim :]
                scores = lax.dot_general(
                    queries, qkv[h, here, dim : 2 * dim], (((1,), (1,)), ((), ())),
                    preferred_element_type=jnp.float32,
                )
                masked = jnp.where(causal, scores, 0.0).astype(jnp.bfloat16)
                mixed = jnp.dot(
                    jnp.concatenate([masked, queries], 1),
                    jnp.concatenate([values, prefix[h, block]], 0),
                    preferred_element_type=jnp.float32,
                )
                spread = lax.rsqrt(row_sums(mixed * mixed) * (1.0 / dim) + epsilon)
                result = (
                    stream[here, mine].astype(jnp.float32)
                    + gains_out[layer, :, mine] * (mixed * spread)
                ).astype(jnp.bfloat16)
                stream[here, mine] = result
                result = result.astype(jnp.float32)
                folded = folded + result * result

            @pl.when(layer < z)
            def _():
                squares[layer + 1, c, pl.ds(block, 1), :] = jnp.sum(folded.T, 0, keepdims=True)

            @pl.when(layer == z)
            def _():
                (out_copy(d) if d else own_out()).start()

        @pl.when(layer < z)
        def _():
            for d in FAR_FIRST:
                sq_copy(layer + 1, d).start()

        for d in FAR_FIRST:
            sq_copy(layer, d).wait_send()
        return carry

    lax.fori_loop(0, z + 1, one_layer, 0)

    own_out().wait()
    for d in FAR_FIRST:
        tok_copy(d).wait_send()
        out_copy(d).wait()
    for stage in plan:
        for sender, layer, to, slot in plan[stage]:
            @pl.when(z == sender)
            def _():
                for copy in w_copies(layer, to, slot, stage == "relay"):
                    copy.wait_send()


def relay(tokens, w_qkv, norm_gain, out_gain):
    ctx_size, sections = lax.axis_size("ctx"), lax.axis_size("pipe")
    rows, features = tokens.shape[1:]
    all_heads, dim = w_qkv.shape[1:3]
    heads = all_heads // ctx_size
    width = heads * dim
    dma = pltpu.SemaphoreType.DMA
    return pl.pallas_call(
        functools.partial(relay_kernel, (ctx_size, sections, heads, dim, rows)),
        out_shape=jax.ShapeDtypeStruct((1,) + tokens.shape, jnp.bfloat16),
        in_specs=[pl.BlockSpec(memory_space=pl.ANY)] * 4,
        out_specs=pl.BlockSpec(memory_space=pl.ANY),
        scratch_shapes=[
            pltpu.VMEM((rows, features), jnp.bfloat16),
            pltpu.VMEM((ctx_size * rows, width), jnp.bfloat16),
            pltpu.VMEM((sections, heads, dim, 3 * dim), jnp.bfloat16),
            pltpu.VMEM((sections, 1, width), jnp.float32),
            pltpu.VMEM((sections, 1, width), jnp.float32),
            pltpu.VMEM((heads, ctx_size * rows, 3 * dim), jnp.bfloat16),
            pltpu.VMEM((heads, ctx_size, dim, dim), jnp.bfloat16),
            pltpu.VMEM((sections, ctx_size, ctx_size, rows), jnp.float32),
            dma((5,)),
            dma((ctx_size,)),
            dma((ctx_size,)),
            dma((sections, ctx_size)),
            dma((sections, ctx_size)),
            dma((sections, 3)),
            dma((sections, 3)),
            dma((ctx_size,)),
            dma((ctx_size,)),
        ],
        compiler_params=pltpu.CompilerParams(collective_id=0, has_side_effects=True),
    )(tokens, w_qkv, norm_gain, out_gain)


def solution(mesh):
    ctx_size, sections = mesh.shape["ctx"], mesh.shape["pipe"]

    def body(tokens, w_qkv, norm_gain, out_gain):
        micro_count, rows = tokens.shape[:2]
        fits = (
            ctx_size == 8
            and sections in (3, 4)
            and micro_count == 1
            and rows == 128
            and w_qkv.shape[1] == 2 * ctx_size
            and w_qkv.shape[2] == 128
        )
        return (relay if fits else shards)(tokens, w_qkv, norm_gain, out_gain)

    placed = (P(None, "ctx", None), P("pipe", None, None, None), P("pipe", None), P("pipe", None))
    return jax.shard_map(
        body, mesh=mesh, in_specs=placed, out_specs=P("pipe", None, "ctx", None), check_vma=False
    )
```

profile of v0, /device:TPU:25, one launch (start us, length us, event | category | flops | bytes accessed | tf_op | source)
XLA Modules:
  0.0 57.8 jit_solution(5143118359189905971)
XLA Ops:
  0.0 55.9 %shard_map.46 = bf16[1,1,128,2048]{3,2,1,0:T(8,128)(2,1)} custom-call(bf16[1,128,2048]{2,1,0:T(8,128)(2,1)} %tok_ref.1, bf16[1,16,128,384]{3,2,1,0:T(8,128)(2,1)} %w_ref.1, f32[1,2048]{1,0:T(1,128)} %gin_ref.1, f32[1,2048]{1,0:T(1,128)} %gout_ref.1), custom_call_target="tpu_custom_call" | custom-call | tf_op jit(solution)/shard_map/pallas_call | solution.py:359
  55.9 1.9 %copy.6 = bf16[1,1,128,2048]{3,2,1,0:T(8,128)(2,1)} copy(bf16[1,1,128,2048]{3,2,1,0:T(8,128)(2,1)} %shard_map.46) | data formatting | bytes 1048576
where the time goes:
time: 57.9 us; the launch traced here: 57.8 us
  Pallas kernels  55.9 us (97%)
  local copies, waits for them, and re-layouts  1.88 us (3%)
    pallas_call x1, Pallas kernels, relay(): pl.pallas_call(functools.partial(relay_kernel, (ctx_size, sections, heads...  55.9 us
    unnamed x1, local copies, waits for them, and re-layouts  1.88 us

commit v1 on v0

--- a/solution.py
+++ b/solution.py
@@ -123,8 +123,12 @@
     weights,
     gains_in,
     gains_out,
-    qkv,
-    prefix,
+    left,
+    right,
+    keys,
+    values,
+    resid,
+    row_scale,
     squares,
     local_sem,
     tok_send,
@@ -265,6 +269,26 @@
         def _():
             send_weights("relay")
 
+        for block in range(ctx_size):
+            here = slice(block * tokens, (block + 1) * tokens)
+            for h in range(heads):
+                mine = slice(h * dim, (h + 1) * dim)
+                entering = stream[here, mine]
+                resid[here, mine] = entering
+                gained = (entering.astype(jnp.float32) * gains_in[layer, :, mine]).astype(
+                    jnp.bfloat16
+                )
+                projected = jnp.dot(
+                    gained, weights[layer, h], preferred_element_type=jnp.float32
+                )
+                queries = projected[:, :dim].astype(jnp.bfloat16)
+                turned = projected[:, dim : 2 * dim].astype(jnp.bfloat16).T
+                scores = jnp.dot(queries, turned, preferred_element_type=jnp.float32)
+                left[h, here, :dim] = jnp.where(causal, scores, 0.0).astype(jnp.bfloat16)
+                left[h, here, dim:] = queries
+                keys[h, block] = turned
+                values[h, here] = projected[:, 2 * dim :]
+
         for d in FAR_FIRST:
             sq_copy(layer, d).wait_recv()
         scale = lax.rsqrt(jnp.sum(squares[layer], 0) * (1.0 / features) + epsilon)
@@ -272,59 +296,40 @@
         for block in range(ctx_size):
             here = slice(block * tokens, (block + 1) * tokens)
             by_row = lanes_to_rows(scale[block : block + 1, :])
+            row_scale[here] = by_row * dim ** (-0.5)
+            twice = by_row * by_row
             for h in range(heads):
-                mine = slice(h * dim, (h + 1) * dim)
-                normed = (
-                    stream[here, mine].astype(jnp.float32) * by_row * gains_in[layer, :, mine]
-                ).astype(jnp.bfloat16)
-                projected = jnp.dot(
-                    normed, weights[layer, h], preferred_element_type=jnp.float32
-                )
-                keys = projected[:, dim : 2 * dim].astype(jnp.bfloat16)
-                values = projected[:, 2 * dim :].astype(jnp.bfloat16)
-                qkv[h, here, :dim] = (projected[:, :dim] * dim ** (-0.5)).astype(jnp.bfloat16)
-                qkv[h, here, dim : 2 * dim] = keys
-                qkv[h, here, 2 * dim :] = values
-                prefix[h, block] = running[h].astype(jnp.bfloat16)
+                scaled = (values[h, here] * twice).astype(jnp.bfloat16)
+                right[h, block, :tokens] = scaled
+                right[h, block, tokens:] = running[h].astype(jnp.bfloat16)
                 if block + 1 < ctx_size:
-                    running[h] = running[h] + lax.dot_general(
-                        keys, values, (((0,), (0,)), ((), ())),
-                        preferred_element_type=jnp.float32,
+                    running[h] = running[h] + jnp.dot(
+                        keys[h, block], scaled, preferred_element_type=jnp.float32
                     )
-        for d in FAR_FIRST + (0,):
-            block = partner(c, d)
-            here = rows(block)
-            folded = jnp.zeros((tokens, dim), jnp.float32)
-            for h in range(heads):
-                mine = slice(h * dim, (h + 1) * dim)
-                queries = qkv[h, here, :dim]
-                values = qkv[h, here, 2 * dim :]
-                scores = lax.dot_general(
-                    queries, qkv[h, here, dim : 2 * dim], (((1,), (1,)), ((), ())),
-                    preferred_element_type=jnp.float32,
-                )
-                masked = jnp.where(causal, scores, 0.0).astype(jnp.bfloat16)
-                mixed = jnp.dot(
-                    jnp.concatenate([masked, queries], 1),
-                    jnp.concatenate([values, prefix[h, block]], 0),
-                    preferred_element_type=jnp.float32,
-                )
-                spread = lax.rsqrt(row_sums(mixed * mixed) * (1.0 / dim) + epsilon)
-                result = (
-                    stream[here, mine].astype(jnp.float32)
-                    + gains_out[layer, :, mine] * (mixed * spread)
-                ).astype(jnp.bfloat16)
-                stream[here, mine] = result
-                result = result.astype(jnp.float32)
-                folded = folded + result * result
-
-            @pl.when(layer < z)
-            def _():
+        for group in (FAR_FIRST[:4], FAR_FIRST[4:] + (0,)):
+            for d in group:
+                block = partner(c, d)
+                here = rows(block)
+                folded = jnp.zeros((tokens, dim), jnp.float32)
+                for h in range(heads):
+                    mine = slice(h * dim, (h + 1) * dim)
+                    mixed = row_scale[here] * jnp.dot(
+                        left[h, here], right[h, block], preferred_element_type=jnp.float32
+                    )
+                    spread = lax.rsqrt(row_sums(mixed * mixed) * (1.0 / dim) + epsilon)
+                    result = (
+                        resid[here, mine].astype(jnp.float32)
+                        + gains_out[layer, :, mine] * (mixed * spread)
+                    ).astype(jnp.bfloat16)
+                    stream[here, mine] = result
+                    result = result.astype(jnp.float32)
+                    folded = folded + result * result
                 squares[layer + 1, c, pl.ds(block, 1), :] = jnp.sum(folded.T, 0, keepdims=True)
 
             @pl.when(layer == z)
             def _():
-                (out_copy(d) if d else own_out()).start()
+                for d in group:
+                    (out_copy(d) if d else own_out()).start()
 
         @pl.when(layer < z)
         def _():
@@ -367,9 +372,13 @@
             pltpu.VMEM((sections, heads, dim, 3 * dim), jnp.bfloat16),
             pltpu.VMEM((sections, 1, width), jnp.float32),
             pltpu.VMEM((sections, 1, width), jnp.float32),
-            pltpu.VMEM((heads, ctx_size * rows, 3 * dim), jnp.bfloat16),
-            pltpu.VMEM((heads, ctx_size, dim, dim), jnp.bfloat16),
-            pltpu.VMEM((sections, ctx_size, ctx_size, rows), jnp.float32),
+            pltpu.VMEM((heads, ctx_size * rows, 2 * dim), jnp.bfloat16),
+            pltpu.VMEM((heads, ctx_size, rows + dim, dim), jnp.bfloat16),
+            pltpu.VMEM((heads, ctx_size, dim, rows), jnp.bfloat16),
+            pltpu.VMEM((heads, ctx_size * rows, dim), jnp.float32),
+            pltpu.VMEM((ctx_size * rows, width), jnp.bfloat16),
+            pltpu.VMEM((ctx_size * rows, dim), jnp.float32),
+            pltpu.VMEM((sections + 1, ctx_size, ctx_size, rows), jnp.float32),
             dma((5,)),
             dma((ctx_size,)),
             dma((ctx_size,)),

time: 57.9 us -> 39.8 us (0.69)
  the two profiles are of different devices: /device:TPU:25 before, /device:TPU:17 now
where the time goes in v1:
time: 39.8 us; the launch traced here: 39.7 us
  Pallas kernels  37.8 us (95%)
  local copies, waits for them, and re-layouts  1.88 us (5%)
    pallas_call x1, Pallas kernels, relay(): pl.pallas_call(functools.partial(relay_kernel, (ctx_size, sections, heads...  37.8 us
    unnamed x1, local copies, waits for them, and re-layouts  1.88 us

profile of v1, /device:TPU:17, one launch (start us, length us, event | category | flops | bytes accessed | tf_op | source)
XLA Modules:
  0.0 39.7 jit_solution(2487025601463081059)
XLA Ops:
  0.0 37.8 %shard_map.46 = bf16[1,1,128,2048]{3,2,1,0:T(8,128)(2,1)} custom-call(bf16[1,128,2048]{2,1,0:T(8,128)(2,1)} %tok_ref.1, bf16[1,16,128,384]{3,2,1,0:T(8,128)(2,1)} %w_ref.1, f32[1,2048]{1,0:T(1,128)} %gin_ref.1, f32[1,2048]{1,0:T(1,128)} %gout_ref.1), custom_call_target="tpu_custom_call" | custom-call | tf_op jit(solution)/shard_map/pallas_call | solution.py:364
  37.8 1.9 %copy.6 = bf16[1,1,128,2048]{3,2,1,0:T(8,128)(2,1)} copy(bf16[1,1,128,2048]{3,2,1,0:T(8,128)(2,1)} %shard_map.46) | data formatting | bytes 1048576

commit v2 on v1

--- a/solution.py
+++ b/solution.py
@@ -187,11 +187,12 @@
         )
 
     def w_copies(layer, to, slot, relayed):
-        pieces = (
-            (weights.at[layer], weights.at[layer]) if relayed else (w_ref.at[0, my_heads], weights.at[layer]),
-            (gains_in.at[layer], gains_in.at[layer]) if relayed else (gin_ref.at[:, cols(c)], gains_in.at[layer]),
-            (gains_out.at[layer], gains_out.at[layer]) if relayed else (gout_ref.at[:, cols(c)], gains_out.at[layer]),
-        )
+        pieces = [
+            (weights.at[layer, h] if relayed else w_ref.at[0, c * heads + h], weights.at[layer, h])
+            for h in range(heads)
+        ]
+        for gain_ref, gain in ((gin_ref, gains_in), (gout_ref, gains_out)):
+            pieces.append((gain.at[layer] if relayed else gain_ref.at[:, cols(c)], gain.at[layer]))
         return [
             pltpu.make_async_remote_copy(
                 source, target, w_send.at[slot, i], w_recv.at[layer, i],
@@ -234,14 +235,31 @@
     squares[0, c] = jnp.where(which == c, jnp.broadcast_to(total, (ctx_size, tokens)), 0.0)
     for d in FAR_FIRST:
         sq_copy(0, d).start()
-    for d in FAR_FIRST[:2]:
+    for d in (1, 6):
         tok_copy(d).wait_recv()
     send_weights("early")
-    for d in FAR_FIRST[2:]:
-        tok_copy(d).wait_recv()
+    tok_copy(7).wait_recv()
     for copy in local[1:]:
         copy.wait()
     send_weights("late")
+
+    def await_weights(layer):
+        for copy in w_copies(layer, z, 0, True):
+            copy.wait_recv()
+
+    @pl.when(jnp.logical_and(z > 0, z < last))
+    def _():
+        await_weights(0)
+
+    @pl.when(z == last)
+    def _():
+        if last > 2:
+            onward = w_copies(0, last - 1, 0, True)
+            for arriving, leaving in zip(w_copies(0, z, 0, True), onward):
+                arriving.wait_recv()
+                leaving.start()
+        else:
+            await_weights(0)
 
     at_row = lax.broadcasted_iota(jnp.int32, (tokens, tokens), 0)
     at_col = lax.broadcasted_iota(jnp.int32, (tokens, tokens), 1)
@@ -259,36 +277,32 @@
             stream.at[rows(c)], out_ref.at[0, 0, :, cols(c)], local_sem.at[0]
         )
 
+    def project(layer, block):
+        here = rows(block)
+        for h in range(heads):
+            mine = slice(h * dim, (h + 1) * dim)
+            entering = stream[here, mine]
+            resid[here, mine] = entering
+            gained = (entering.astype(jnp.float32) * gains_in[layer, :, mine]).astype(
+                jnp.bfloat16
+            )
+            projected = jnp.dot(gained, weights[layer, h], preferred_element_type=jnp.float32)
+            queries = projected[:, :dim].astype(jnp.bfloat16)
+            turned = projected[:, dim : 2 * dim].astype(jnp.bfloat16).T
+            scores = jnp.dot(queries, turned, preferred_element_type=jnp.float32)
+            left[h, here, :dim] = jnp.where(causal, scores, 0.0).astype(jnp.bfloat16)
+            left[h, here, dim:] = queries
+            keys[h, block] = turned
+            values[h, here] = projected[:, 2 * dim :]
+
+    for pair in ((0, 1), (6, 7), (2, 4), (3, 5)):
+        for d in pair:
+            if d in (2, 3, 4, 5):
+                tok_copy(d).wait_recv()
+        for d in pair:
+            project(0, partner(c, d))
+
     def one_layer(layer, carry):
-        @pl.when(layer < z)
-        def _():
-            for copy in w_copies(layer, z, 0, True):
-                copy.wait_recv()
-
-        @pl.when(layer == 0)
-        def _():
-            send_weights("relay")
-
-        for block in range(ctx_size):
-            here = slice(block * tokens, (block + 1) * tokens)
-            for h in range(heads):
-                mine = slice(h * dim, (h + 1) * dim)
-                entering = stream[here, mine]
-                resid[here, mine] = entering
-                gained = (entering.astype(jnp.float32) * gains_in[layer, :, mine]).astype(
-                    jnp.bfloat16
-                )
-                projected = jnp.dot(
-                    gained, weights[layer, h], preferred_element_type=jnp.float32
-                )
-                queries = projected[:, :dim].astype(jnp.bfloat16)
-                turned = projected[:, dim : 2 * dim].astype(jnp.bfloat16).T
-                scores = jnp.dot(queries, turned, preferred_element_type=jnp.float32)
-                left[h, here, :dim] = jnp.where(causal, scores, 0.0).astype(jnp.bfloat16)
-                left[h, here, dim:] = queries
-                keys[h, block] = turned
-                values[h, here] = projected[:, 2 * dim :]
-
         for d in FAR_FIRST:
             sq_copy(layer, d).wait_recv()
         scale = lax.rsqrt(jnp.sum(squares[layer], 0) * (1.0 / features) + epsilon)
@@ -336,6 +350,13 @@
             for d in FAR_FIRST:
                 sq_copy(layer + 1, d).start()
 
+            @pl.when(layer + 1 < z)
+            def _():
+                await_weights(layer + 1)
+
+            for block in range(ctx_size):
+                project(layer + 1, block)
+
         for d in FAR_FIRST:
             sq_copy(layer, d).wait_send()
         return carry
@@ -384,8 +405,8 @@
             dma((ctx_size,)),
             dma((sections, ctx_size)),
             dma((sections, ctx_size)),
-            dma((sections, 3)),
-            dma((sections, 3)),
+            dma((sections, heads + 2)),
+            dma((sections, heads + 2)),
             dma((ctx_size,)),
             dma((ctx_size,)),
         ],

time: 39.8 us -> 38.1 us (0.957)
  Pallas kernels: 37.8 us -> 36.1 us
    pallas_call x1, Pallas kernels: 37.8 us -> 36.1 us  [relay(): pl.pallas_call(functools.partial(relay_kernel, (ctx_size, sections, heads...]
where the time goes in v2:
time: 38.1 us; the launch traced here: 38 us
  Pallas kernels  36.1 us (95%)
  local copies, waits for them, and re-layouts  1.88 us (5%)
    pallas_call x1, Pallas kernels, relay(): pl.pallas_call(functools.partial(relay_kernel, (ctx_size, sections, heads...  36.1 us
    unnamed x1, local copies, waits for them, and re-layouts  1.88 us

profile of v2, /device:TPU:17, one launch (start us, length us, event | category | flops | bytes accessed | tf_op | source)
XLA Modules:
  0.0 38.0 jit_solution(15394288015684160700)
XLA Ops:
  0.0 36.1 %shard_map.46 = bf16[1,1,128,2048]{3,2,1,0:T(8,128)(2,1)} custom-call(bf16[1,128,2048]{2,1,0:T(8,128)(2,1)} %tok_ref.1, bf16[1,16,128,384]{3,2,1,0:T(8,128)(2,1)} %w_ref.1, f32[1,2048]{1,0:T(1,128)} %gin_ref.1, f32[1,2048]{1,0:T(1,128)} %gout_ref.1), custom_call_target="tpu_custom_call" | custom-call | tf_op jit(solution)/shard_map/pallas_call | solution.py:385
  36.1 1.9 %copy.6 = bf16[1,1,128,2048]{3,2,1,0:T(8,128)(2,1)} copy(bf16[1,1,128,2048]{3,2,1,0:T(8,128)(2,1)} %shard_map.46) | data formatting | bytes 1048576
